TPU v7x, 32 devices: a whole 2x2x4 slice. The times are simulated.
32 devices in a mesh: dp: 16 (over z, y, core), fsdp: 2 (over x).
Axes of the slice: x: 2, y: 2, z: 4, core: 2. Of those that a mesh axis runs over, the one named last changes fastest.
Arguments:
- latents: bfloat16 [32768, 768], P(('dp', 'fsdp')), may hold values from -6 to 6
- size_tags: int32 [32], P(('dp', 'fsdp')), may hold values from 0 to 1
- timesteps: int32 [32, 4], P(('dp', 'fsdp')), may hold values from 0 to 999
- classes: int32 [32, 4], P(('dp', 'fsdp')), may hold values from 0 to 999
- step_table: bfloat16 [1000, 768], P('fsdp', 'dp'), may hold values from -5 to 5
- class_table: bfloat16 [1000, 768], P('fsdp', 'dp'), may hold values from -5 to 5
- modulation_weight: bfloat16 [768, 4608], P('fsdp', 'dp'), may hold values from -0.21875 to 0.21875
- attn_kernel: bfloat16 [9, 768], P(None, 'dp'), may hold values from -2 to 2
- qkv_weight: bfloat16 [768, 2304], P('fsdp', 'dp'), may hold values from -0.21875 to 0.21875
- proj_weight: bfloat16 [768, 768], P('fsdp', 'dp'), may hold values from -1.75 to 1.75
- expand_weight: bfloat16 [768, 3072], P('fsdp', 'dp'), may hold values from -0.21875 to 0.21875
- ffn_kernel: bfloat16 [9, 3072], P(None, 'dp'), may hold values from -2 to 2
- shrink_weight: bfloat16 [3072, 768], P('fsdp', 'dp'), may hold values from -0.109375 to 0.109375
- cotangent: bfloat16 [32768, 768], P(('dp', 'fsdp')), may hold values from -6 to 6
Outputs:
- block_output: bfloat16 [32768, 768], P(('dp', 'fsdp'))
- input_grad: float32 [32768, 768], P(('dp', 'fsdp'))
- step_table_grad: float32 [1000, 768], P('fsdp', 'dp')
- class_table_grad: float32 [1000, 768], P('fsdp', 'dp')
- modulation_grad: float32 [768, 4608], P('fsdp', 'dp')
- attn_kernel_grad: float32 [9, 768], P(None, 'dp')
- qkv_grad: float32 [768, 2304], P('fsdp', 'dp')
- proj_grad: float32 [768, 768], P('fsdp', 'dp')
- expand_grad: float32 [768, 3072], P('fsdp', 'dp')
- ffn_kernel_grad: float32 [9, 3072], P(None, 'dp')
- shrink_grad: float32 [3072, 768], P('fsdp', 'dp')
Inputs may be any that keep to these rules, and one draw needn't show every extreme that they name: `size_tags`: a slot with tag 0 holds one item of 1024 tokens, with tag 1 four items of 16 x 16 tokens. `timesteps`: in a slot with tag 0 only entry 0 is used. `classes`: in a slot with tag 0 only entry 0 is used.
All inputs are finite; a program needn't handle non-finite values.
Results may differ from a plain program's by a relative error of at most 0.019.
The roundings to bfloat16 on the way count: a program that leaves them out, or rounds other values in their place, can miss the bound.
Values may be sent and summed in bfloat16 or wider, within the bound.
No kernel may reach another device: no remote copies, remote signals or barrier semaphores. Data moves between devices by JAX's collectives and lax.ppermute only.
A program may use at most 384 MiB of HBM per device.

v0:
```python
import jax
import jax.numpy as jnp
from jax import lax
from jax.sharding import PartitionSpec as P

D = 768
H = 12
HD = 64
STEPS = 1000
CLASSES = 1000
SIDE = 32
GROUP = 256


def token_items(size_tag):
    row_index = jnp.arange(SIDE, dtype=jnp.int32)
    quadrant = row_index // (SIDE // 2)
    layout = quadrant[:, None] * 2 + quadrant[None, :]
    return (layout * size_tag).reshape(SIDE * SIDE)


def edge_masks(size_tag):
    row_index = jnp.arange(SIDE, dtype=jnp.int32)
    half_side = SIDE // 2
    collected = []
    for offset in (-1, 0, 1):
        neighbour = row_index + offset
        inside = (neighbour >= 0) & (neighbour < SIDE)
        same_item = jnp.maximum(neighbour, 0) // half_side == row_index // half_side
        collected.append((inside & (same_item | (size_tag == 0))).astype(jnp.float32))
    return collected


def depthwise(field, kernel, validity):
    channels = field.shape[-1]
    layout = field.reshape(SIDE, SIDE, channels)
    padded = jnp.pad(layout, ((1, 1), (1, 1), (0, 0)))
    summed = jnp.zeros_like(layout)
    for row_step in range(3):
        for col_step in range(3):
            window = padded[row_step : row_step + SIDE, col_step : col_step + SIDE]
            allowed = validity[row_step][:, None] * validity[col_step][None, :]
            summed = summed + window * allowed[:, :, None] * kernel[row_step * 3 + col_step]
    return summed.reshape(SIDE * SIDE, channels)


def to_groups(field):
    channels = field.shape[-1]
    layout = field.reshape(SIDE // 2, 2, SIDE // 2, 2, channels)
    return layout.transpose(1, 3, 0, 2, 4).reshape(4, GROUP, channels)


def from_groups(field):
    channels = field.shape[-1]
    layout = field.reshape(2, 2, SIDE // 2, SIDE // 2, channels)
    return layout.transpose(2, 0, 3, 1, 4).reshape(SIDE * SIDE, channels)


def same_item_mask(size_tag):
    position = jnp.arange(SIDE // 2, dtype=jnp.int32) // (SIDE // 4)
    labels = ((position[:, None] * 2 + position[None, :]) * size_tag).reshape(GROUP)
    return labels[:, None] == labels[None, :]


def normalize(values):
    centre = values - jnp.mean(values, axis=-1, keepdims=True)
    variance = jnp.mean(centre * centre, axis=-1, keepdims=True)
    return centre * lax.rsqrt(variance + 1e-06)


def modulate(values, offset_rows, scale_rows):
    return normalize(values) * (1.0 + scale_rows) + offset_rows


def per_token(mod_rows, labels):
    pieces = []
    for component in range(6):
        column = mod_rows[:, component * D : (component + 1) * D]
        chosen = column[0][None, :] * jnp.ones((labels.shape[0], 1), jnp.float32)
        for other_item in range(1, 4):
            chosen = jnp.where((labels == other_item)[:, None], column[other_item][None, :], chosen)
        pieces.append(chosen)
    return tuple(pieces)


def smooth_gate(values):
    return jax.nn.gelu(values, approximate=True)


def cross(left, right):
    return lax.dot_general(
        left, right, (((0,), (0,)), ((), ())), preferred_element_type=jnp.float32
    )


def against(left, right):
    return lax.dot_general(
        left, right, (((1,), (1,)), ((), ())), preferred_element_type=jnp.float32
    )


def attention_scores(queries, key_rows, allowed):
    scores = jnp.einsum(
        "gqhd,gkhd->ghqk", queries, key_rows, preferred_element_type=jnp.float32
    ) * HD ** (-0.5)
    return jnp.where(allowed[None, None], scores, -1e30)


def fetch_forward(
    step_table,
    class_table,
    modulation_weight,
    qkv_weight,
    proj_weight,
    expand_weight,
    shrink_weight,
    attn_kernel,
    ffn_kernel,
):
    gathered = (
        lax.all_gather(step_table, "fsdp", axis=0, tiled=True),
        lax.all_gather(class_table, "fsdp", axis=0, tiled=True),
        lax.all_gather(modulation_weight, "fsdp", axis=0, tiled=True),
        lax.all_gather(qkv_weight, "fsdp", axis=0, tiled=True),
        lax.all_gather(proj_weight, "fsdp", axis=0, tiled=True),
        lax.all_gather(expand_weight, "fsdp", axis=0, tiled=True),
        lax.all_gather(shrink_weight, "fsdp", axis=0, tiled=True),
    )
    return (
        lax.all_gather(gathered[0], "dp", axis=1, tiled=True),
        lax.all_gather(gathered[1], "dp", axis=1, tiled=True),
        lax.all_gather(gathered[2], "dp", axis=1, tiled=True),
        lax.all_gather(gathered[3], "dp", axis=1, tiled=True),
        lax.all_gather(gathered[4], "dp", axis=1, tiled=True),
        lax.all_gather(gathered[5], "dp", axis=1, tiled=True),
        lax.all_gather(gathered[6], "dp", axis=1, tiled=True),
        lax.all_gather(attn_kernel, "dp", axis=1, tiled=True),
        lax.all_gather(ffn_kernel, "dp", axis=1, tiled=True),
    )


def fetch_again(modulation_weight, qkv_weight, proj_weight, expand_weight, shrink_weight):
    gathered = (
        lax.all_gather(modulation_weight, "fsdp", axis=0, tiled=True),
        lax.all_gather(qkv_weight, "fsdp", axis=0, tiled=True),
        lax.all_gather(proj_weight, "fsdp", axis=0, tiled=True),
        lax.all_gather(expand_weight, "fsdp", axis=0, tiled=True),
        lax.all_gather(shrink_weight, "fsdp", axis=0, tiled=True),
    )
    return (
        lax.all_gather(gathered[0], "dp", axis=1, tiled=True),
        lax.all_gather(gathered[1], "dp", axis=1, tiled=True),
        lax.all_gather(gathered[2], "dp", axis=1, tiled=True),
        lax.all_gather(gathered[3], "dp", axis=1, tiled=True),
        lax.all_gather(gathered[4], "dp", axis=1, tiled=True),
    )


def body(
    latents,
    size_tags,
    timesteps,
    classes,
    step_table,
    class_table,
    modulation_weight,
    attn_kernel,
    qkv_weight,
    proj_weight,
    expand_weight,
    ffn_kernel,
    shrink_weight,
    cotangent,
):
    (
        step_full,
        class_full,
        mod_full,
        qkv_full,
        proj_full,
        expand_full,
        shrink_full,
        attn_full,
        ffn_full,
    ) = fetch_forward(
        step_table,
        class_table,
        modulation_weight,
        qkv_weight,
        proj_weight,
        expand_weight,
        shrink_weight,
        attn_kernel,
        ffn_kernel,
    )
    size_tag = size_tags[0]
    steps_hot = (timesteps[0][:, None] == jnp.arange(STEPS, dtype=jnp.int32)[None, :]).astype(
        jnp.float32
    )
    class_hot = (classes[0][:, None] == jnp.arange(CLASSES, dtype=jnp.int32)[None, :]).astype(
        jnp.float32
    )
    cond = jnp.dot(
        steps_hot.astype(jnp.bfloat16), step_full, preferred_element_type=jnp.float32
    ) + jnp.dot(class_hot.astype(jnp.bfloat16), class_full, preferred_element_type=jnp.float32)
    activated, silu_back = jax.vjp(jax.nn.silu, cond)
    act_low = activated.astype(jnp.bfloat16)
    mod_rows = jnp.dot(act_low, mod_full, preferred_element_type=jnp.float32)
    labels = token_items(size_tag)

    def spread_rows(rows):
        return per_token(rows, labels)

    (shift_one, scale_one, gate_one, shift_two, scale_two, gate_two), spread_back = jax.vjp(
        spread_rows, mod_rows
    )
    validity = edge_masks(size_tag)
    allowed = same_item_mask(size_tag)

    def conv_pass(field, kernel):
        return depthwise(field, kernel, validity)

    inputs = latents.astype(jnp.float32)
    first, first_back = jax.vjp(modulate, inputs, shift_one, scale_one)
    conv_out, conv_one_back = jax.vjp(conv_pass, first, attn_full.astype(jnp.float32))
    conv_low = conv_out.astype(jnp.bfloat16)
    qkv_low = jnp.dot(conv_low, qkv_full, preferred_element_type=jnp.float32).astype(jnp.bfloat16)
    grouped = to_groups(qkv_low).reshape(4, GROUP, 3, H, HD)
    queries = grouped[:, :, 0]
    key_rows = grouped[:, :, 1]
    value_rows = grouped[:, :, 2]
    scores = attention_scores(queries, key_rows, allowed)
    highest = jnp.max(scores, axis=-1, keepdims=True)
    raised = jnp.exp(scores - highest)
    totals = jnp.sum(raised, axis=-1, keepdims=True)
    probs_low = (raised / totals).astype(jnp.bfloat16)
    log_total = highest + jnp.log(totals)
    mixed = jnp.einsum("ghqk,gkhd->gqhd", probs_low, value_rows, preferred_element_type=jnp.float32)
    merged_low = from_groups(mixed.reshape(4, GROUP, D)).astype(jnp.bfloat16)
    attn = jnp.dot(merged_low, proj_full, preferred_element_type=jnp.float32)
    resid = inputs + gate_one * attn
    second, second_back = jax.vjp(modulate, resid, shift_two, scale_two)
    second_low = second.astype(jnp.bfloat16)
    expanded = jnp.dot(second_low, expand_full, preferred_element_type=jnp.float32)
    conved, conv_two_back = jax.vjp(conv_pass, expanded, ffn_full.astype(jnp.float32))
    hidden, gate_back = jax.vjp(smooth_gate, conved)
    hidden_low = hidden.astype(jnp.bfloat16)
    shrunk = jnp.dot(hidden_low, shrink_full, preferred_element_type=jnp.float32)
    block_output = (resid + gate_two * shrunk).astype(jnp.bfloat16)
    mod_back, qkv_back, proj_back, expand_back, shrink_back = fetch_again(
        modulation_weight, qkv_weight, proj_weight, expand_weight, shrink_weight
    )
    d_out = cotangent.astype(jnp.float32)
    d_gate_two = d_out * shrunk
    d_shrunk = (gate_two * d_out).astype(jnp.bfloat16)
    shrink_term = cross(hidden_low, d_shrunk)
    (d_conved,) = gate_back(against(d_shrunk, shrink_back))
    d_expanded, ffn_term = conv_two_back(d_conved)
    d_expanded_low = d_expanded.astype(jnp.bfloat16)
    expand_term = cross(second_low, d_expanded_low)
    d_resid_norm, d_shift_two, d_scale_two = second_back(against(d_expanded_low, expand_back))
    d_resid = d_out + d_resid_norm
    d_gate_one = d_resid * attn
    d_attn = (gate_one * d_resid).astype(jnp.bfloat16)
    proj_term = cross(merged_low, d_attn)
    d_merged = against(d_attn, proj_back).astype(jnp.bfloat16)
    d_mixed = to_groups(d_merged).reshape(4, GROUP, H, HD)
    probs_again = jnp.exp(attention_scores(queries, key_rows, allowed) - log_total)
    probs_again_low = probs_again.astype(jnp.bfloat16)
    d_values = jnp.einsum(
        "ghqk,gqhd->gkhd", probs_again_low, d_mixed, preferred_element_type=jnp.float32
    )
    d_probs = jnp.einsum("gqhd,gkhd->ghqk", d_mixed, value_rows, preferred_element_type=jnp.float32)
    inner = jnp.sum(probs_again * d_probs, axis=-1, keepdims=True)
    d_scores = (probs_again * (d_probs - inner)).astype(jnp.bfloat16)
    d_queries = jnp.einsum(
        "ghqk,gkhd->gqhd", d_scores, key_rows, preferred_element_type=jnp.float32
    ) * HD ** (-0.5)
    d_keys = jnp.einsum(
        "ghqk,gqhd->gkhd", d_scores, queries, preferred_element_type=jnp.float32
    ) * HD ** (-0.5)
    stacked = jnp.stack([d_queries, d_keys, d_values], axis=2).reshape(4, GROUP, 3 * D)
    d_qkv = from_groups(stacked).astype(jnp.bfloat16)
    qkv_term = cross(conv_low, d_qkv)
    d_first, attn_term = conv_one_back(against(d_qkv, qkv_back))
    d_input_norm, d_shift_one, d_scale_one = first_back(d_first)
    input_grad = d_resid + d_input_norm
    (d_mod,) = spread_back(
        (d_shift_one, d_scale_one, d_gate_one, d_shift_two, d_scale_two, d_gate_two)
    )
    d_mod_low = d_mod.astype(jnp.bfloat16)
    (d_cond,) = silu_back(against(d_mod_low, mod_back))
    mod_term = cross(act_low, d_mod_low)
    step_term = lax.dot_general(
        steps_hot, d_cond, (((0,), (0,)), ((), ())), precision=lax.Precision.HIGHEST
    )
    class_term = lax.dot_general(
        class_hot, d_cond, (((0,), (0,)), ((), ())), precision=lax.Precision.HIGHEST
    )
    (
        step_cols,
        class_cols,
        mod_cols_sum,
        qkv_cols,
        proj_cols,
        expand_cols,
        shrink_cols,
        attn_kernel_part,
        ffn_kernel_part,
    ) = (
        lax.psum_scatter(
            step_term.astype(jnp.bfloat16), "dp", scatter_dimension=1, tiled=True
        ).astype(jnp.float32),
        lax.psum_scatter(
            class_term.astype(jnp.bfloat16), "dp", scatter_dimension=1, tiled=True
        ).astype(jnp.float32),
        lax.psum_scatter(
            mod_term.astype(jnp.bfloat16), "dp", scatter_dimension=1, tiled=True
        ).astype(jnp.float32),
        lax.psum_scatter(
            qkv_term.astype(jnp.bfloat16), "dp", scatter_dimension=1, tiled=True
        ).astype(jnp.float32),
        lax.psum_scatter(
            proj_term.astype(jnp.bfloat16), "dp", scatter_dimension=1, tiled=True
        ).astype(jnp.float32),
        lax.psum_scatter(
            expand_term.astype(jnp.bfloat16), "dp", scatter_dimension=1, tiled=True
        ).astype(jnp.float32),
        lax.psum_scatter(
            shrink_term.astype(jnp.bfloat16), "dp", scatter_dimension=1, tiled=True
        ).astype(jnp.float32),
        lax.psum_scatter(
            attn_term.astype(jnp.bfloat16), "dp", scatter_dimension=1, tiled=True
        ).astype(jnp.float32),
        lax.psum_scatter(
            ffn_term.astype(jnp.bfloat16), "dp", scatter_dimension=1, tiled=True
        ).astype(jnp.float32),
    )
    step_grad, class_grad, mod_grad, qkv_grad, proj_grad, expand_grad, shrink_grad = (
        lax.psum_scatter(
            step_cols.astype(jnp.bfloat16), "fsdp", scatter_dimension=0, tiled=True
        ).astype(jnp.float32),
        lax.psum_scatter(
            class_cols.astype(jnp.bfloat16), "fsdp", scatter_dimension=0, tiled=True
        ).astype(jnp.float32),
        lax.psum_scatter(
            mod_cols_sum.astype(jnp.bfloat16), "fsdp", scatter_dimension=0, tiled=True
        ).astype(jnp.float32),
        lax.psum_scatter(
            qkv_cols.astype(jnp.bfloat16), "fsdp", scatter_dimension=0, tiled=True
        ).astype(jnp.float32),
        lax.psum_scatter(
            proj_cols.astype(jnp.bfloat16), "fsdp", scatter_dimension=0, tiled=True
        ).astype(jnp.float32),
        lax.psum_scatter(
            expand_cols.astype(jnp.bfloat16), "fsdp", scatter_dimension=0, tiled=True
        ).astype(jnp.float32),
        lax.psum_scatter(
            shrink_cols.astype(jnp.bfloat16), "fsdp", scatter_dimension=0, tiled=True
        ).astype(jnp.float32),
    )
    attn_kernel_grad, ffn_kernel_grad = lax.psum((attn_kernel_part, ffn_kernel_part), "fsdp")
    return (
        block_output,
        input_grad,
        step_grad,
        class_grad,
        mod_grad,
        attn_kernel_grad,
        qkv_grad,
        proj_grad,
        expand_grad,
        ffn_kernel_grad,
        shrink_grad,
    )


def solution(mesh):
    in_specs = (
        P(("dp", "fsdp"), None),
        P(("dp", "fsdp")),
        P(("dp", "fsdp"), None),
        P(("dp", "fsdp"), None),
        P("fsdp", "dp"),
        P("fsdp", "dp"),
        P("fsdp", "dp"),
        P(None, "dp"),
        P("fsdp", "dp"),
        P("fsdp", "dp"),
        P("fsdp", "dp"),
        P(None, "dp"),
        P("fsdp", "dp"),
        P(("dp", "fsdp"), None),
    )
    out_specs = (
        P(("dp", "fsdp"), None),
        P(("dp", "fsdp"), None),
        P("fsdp", "dp"),
        P("fsdp", "dp"),
        P("fsdp", "dp"),
        P(None, "dp"),
        P("fsdp", "dp"),
        P("fsdp", "dp"),
        P("fsdp", "dp"),
        P(None, "dp"),
        P("fsdp", "dp"),
    )
    return jax.shard_map(body, mesh=mesh, in_specs=in_specs, out_specs=out_specs, check_vma=False)
```

profile of v0, /device:TPU:0, one launch (start us, length us, event | category | flops | bytes accessed | tf_op | source)
XLA Modules:
  0.0 1364.5 jit_solution(2046139072494940579)
XLA Ops:
  56.5 21.9 %all-gather.2 = bf16[16,48,9]{1,2,0:T(8,128)(2,1)S(1)} all-gather(bf16[1,48,9]{1,2,0:T(8,128)(2,1)S(1)} %bitcast.230), channel_id=1, replica_groups=mesh['dp'=16,'fsdp'=2] {'dp'}, dimensions={0}, use_global_device_ids=true | all-gather | bytes 14688 | tf_op jit(solution)/shard_map/all_gather | solution.py:137
  78.7 17.9 %all-gather.3 = bf16[16,192,9]{1,2,0:T(8,128)(2,1)S(1)} all-gather(bf16[1,192,9]{1,2,0:T(8,128)(2,1)S(1)} %bitcast.229), channel_id=1, replica_groups=mesh['dp'=16,'fsdp'=2] {'dp'}, dimensions={0}, use_global_device_ids=true | all-gather | bytes 58752 | tf_op jit(solution)/shard_map/all_gather | solution.py:138
  101.4 63.7 %all-gather.16.cloned.1.call-done = bf16[768,4608]{0,1:T(8,128)(2,1)} async-done(((bf16[768,288]{0,1:T(8,128)(2,1)}), bf16[768,4608]{0,1:T(8,128)(2,1)}) %all-gather.16.cloned.1.call-update) | async-done | bytes 7077904 | tf_op jit(solution)/shard_map/all_gather | solution.py:132
  183.6 29.4 %all-gather.18.cloned.1.call-done = bf16[768,2304]{0,1:T(8,128)(2,1)} async-done(((bf16[768,144]{0,1:T(8,128)(2,1)}), bf16[768,2304]{0,1:T(8,128)(2,1)}) %all-gather.18.cloned.1.call-update) | async-done | bytes 3538960 | tf_op jit(solution)/shard_map/all_gather | solution.py:133
  235.8 14.9 %reshape_reshape.8 = bf16[4,256,3,12,64]{4,3,2,1,0:T(8,128)(2,1)} reshape(bf16[2,2,16,16,2304]{4,3,2,1,0:T(8,128)(2,1)} %bitcast.186) | data formatting | bytes 9437184 | tf_op jit(solution)/shard_map/reshape;reshape | solution.py:228
  321.5 22.1 %multiply_add_fusion = f32[32,32,3072]{2,1,0:T(8,128)} fusion(f32[32,32,3072]{2,1,0:T(8,128)S(1)} %bitcast.180, f32[3072]{0:T(1024)S(1)} %bitcast.200, f32[32,32]{1,0:T(8,128)S(1)} %get-tuple-element.159, f32[3072]{0:T(1024)S(1)} %bitcast.202, f32[32,32]{1,0:T(8,128)S(1)} %get-tuple-element.154, f32[3072]{0:T(1024)S(1)} %bitcast.204, ...), kind=kLoop, calls=%fused_computation.57 | loop fusion | flops 81788928 | bytes 25313280 | tf_op jit(solution)/shard_map/jvp()/add | solution.py:43
  361.3 63.2 %multiply_reduce_fusion.8 = (f32[3072]{0:T(1024)}, f32[3072]{0:T(1024)}, f32[3072]{0:T(1024)}, f32[3072]{0:T(1024)}, f32[3072]{0:T(1024)}, /*index=5*/f32[3072]{...) fusion(f32[32,32,3072]{2,1,0:T(8,128)} %bitcast.181, f32[32,32]{1,0:T(8,128)S(1)} %get-tuple-element.159, ...), kind=kOutput, calls=%fused_computation.44 | convolution fusion | flops 4971798528 | bytes 44186624 | tf_op jit(solution)/shard_map/dot_general | solution.py:97
  424.6 42.0 %multiply_multiply_fusion.10 = (f32[32,32,3072]{2,1,0:T(8,128)}, f32[32,32,3072]{2,1,0:T(8,128)}, f32[32,32,3072]{2,1,0:T(8,128)}, f32[32,32,3072]{2,1,0:T(8,128...) fusion(f32[32,32,3072]{2,1,0:T(8,128)} %bitcast.179, ...), kind=kLoop, calls=%fused_computation.56 | loop fusion | flops 56623104 | bytes 125976576 | tf_op jit(solution)/shard_map/transpose(jvp())/mul | solution.py:43
  466.6 23.6 %pad_add_fusion = f32[34,34,3072]{2,1,0:T(8,128)} fusion(f32[32,32,3072]{2,1,0:T(8,128)} %get-tuple-element.116, f32[32,32,3072]{2,1,0:T(8,128)} %get-tuple-element.117, f32[32,32,3072]{2,1,0:T(8,128)} %get-tuple-element.118, f32[32,32,3072]{2,1,0:T(8,128)} %get-tuple-element.110), kind=kLoop, calls=%fused_computation.10 | loop fusion | flops 10653696 | bytes 64536576 | tf_op jit(solution)/shard_map/transpose(jvp())/add_any | solution.py:41
  490.2 31.5 %fusion.14 = bf16[32,32,3072]{2,1,0:T(8,128)(2,1)} fusion(f32[32,32,3072]{2,1,0:T(8,128)} %get-tuple-element.111, f32[32,32,3072]{2,1,0:T(8,128)} %get-tuple-element.112, f32[32,32,3072]{2,1,0:T(8,128)} %get-tuple-element.113, f32[32,32,3072]{2,1,0:T(8,128)} %get-tuple-element.114, f32[32,32,3072]{2,1,0:T(8,128)} %get-tuple-element.115, ...), kind=kLoop, calls=%fused_computation.26 | loop fusion | flops 18874368 | bytes 81788928 | tf_op jit(solution)/shard_map/convert
  603.8 15.1 %copy.106 = bf16[4,256,3,12,64]{4,3,2,1,0:T(8,128)(2,1)} copy(bf16[4,256,3,12,64]{1,4,3,0,2:T(8,128)(2,1)} %maximum_convert_fusion) | data formatting | bytes 9437184 | tf_op jit(solution)/shard_map/convert_element_type | solution.py:283
  618.9 15.7 %convert_element_type.240 = bf16[2,2,16,16,2304]{4,3,2,1,0:T(8,128)(2,1)} reshape(bf16[4,256,3,12,64]{4,3,2,1,0:T(8,128)(2,1)} %copy.106) | data formatting | bytes 9437184 | tf_op jit(solution)/shard_map/convert_element_type | solution.py:283
  654.7 14.1 %multiply_multiply_fusion.19 = (f32[32,32,768]{2,1,0:T(8,128)}, f32[32,32,768]{2,1,0:T(8,128)S(1)}, f32[32,32,768]{2,1,0:T(8,128)S(1)}, f32[32,32,768]{2,1,0:T(8...) fusion(f32[768]{0:T(1024)S(1)} %copy-done.69, ...), kind=kOutput, calls=%fused_computation.160 | convolution fusion | flops 3638034432 | bytes 39779328 | tf_op jit(solution)/shard_map/dot_general | solution.py:97
  747.9 18.9 %multiply_reduce_fusion.18 = (f32[768]{0:T(1024)S(1)}, f32[768]{0:T(1024)S(1)}, f32[768]{0:T(1024)S(1)}, f32[768]{0:T(1024)S(1)}, f32[768]{0:T(1024)S(1)}, /*ind...) fusion(f32[32,32,768]{2,1,0:T(8,128)} %get-tuple-element.167, f32[32,32,768]{2,1,0:T(8,128)} %bitcast.183, ...), kind=kLoop, calls=%fused_computation.126 | loop fusion | flops 30663936 | bytes 7964672 | tf_op jit(solution)/shard_map/transpose(jvp())/reduce_sum | solution.py:43
  781.3 35.6 %reduce-scatter.29.cloned.1.call-done = bf16[1000,48]{0,1:T(8,128)(2,1)} async-done(((bf16[1000,768]{0,1:T(8,128)(2,1)}), bf16[1000,48]{0,1:T(8,128)(2,1)}) %reduce-scatter.29.cloned.1.call-update) | async-done | bytes 96016 | tf_op jit(solution)/shard_map/reduce_scatter | solution.py:311
  816.9 70.9 %reduce-scatter.35.cloned.1.call-done = bf16[768,144]{0,1:T(8,128)(2,1)} async-done(((bf16[768,2304]{0,1:T(8,128)(2,1)}), bf16[768,144]{0,1:T(8,128)(2,1)}) %reduce-scatter.35.cloned.1.call-update) | async-done | bytes 221200 | tf_op jit(solution)/shard_map/reduce_scatter | solution.py:320
  889.7 76.3 %reduce-scatter.39.cloned.1.call-done = bf16[768,192]{0,1:T(8,128)(2,1)} async-done(((bf16[768,3072]{0,1:T(8,128)(2,1)}), bf16[768,192]{0,1:T(8,128)(2,1)}) %reduce-scatter.39.cloned.1.call-update) | async-done | bytes 294928 | tf_op jit(solution)/shard_map/reduce_scatter | solution.py:326
  969.3 75.8 %reduce-scatter.41.cloned.1.call-done = bf16[3072,48]{0,1:T(8,128)(2,1)} async-done(((bf16[3072,768]{0,1:T(8,128)(2,1)}), bf16[3072,48]{0,1:T(8,128)(2,1)}) %reduce-scatter.41.cloned.1.call-update) | async-done | bytes 294928 | tf_op jit(solution)/shard_map/reduce_scatter | solution.py:329
  1050.6 87.5 %reduce-scatter.33.cloned.1.call-done = bf16[768,288]{0,1:T(8,128)(2,1)} async-done(((bf16[768,4608]{0,1:T(8,128)(2,1)}), bf16[768,288]{0,1:T(8,128)(2,1)}) %reduce-scatter.33.cloned.1.call-update) | async-done | bytes 442384 | tf_op jit(solution)/shard_map/reduce_scatter | solution.py:317
  1145.3 50.3 %reduce-scatter.47.cloned.1.call-done = bf16[48,9]{1,0:T(8,128)(2,1)} async-done(((bf16[768,9]{1,0:T(8,128)(2,1)}), bf16[48,9]{1,0:T(8,128)(2,1)}) %reduce-scatter.47.cloned.1.call-update) | async-done | bytes 880
  1196.3 58.7 %reduce-scatter.55.cloned.1.call-done = bf16[192,9]{1,0:T(8,128)(2,1)} async-done(((bf16[3072,9]{1,0:T(8,128)(2,1)}), bf16[192,9]{1,0:T(8,128)(2,1)}) %reduce-scatter.55.cloned.1.call-update) | async-done | bytes 3472
  1269.3 23.1 %all-reduce.74.cloned.1.call-done = (bf16[1000,48]{0,1:T(8,128)(2,1)}, bf16[1000,48]{0,1:T(8,128)(2,1)}) async-done(((bf16[1000,48]{0,1:T(8,128)(2,1)}, bf16[1000,48]{0,1:T(8,128)(2,1)}), (bf16[1000,48]{0,1:T(8,128)(2,1)}, bf16[1000,48]{0,1:T(8,128)(2,1)})) %all-reduce.74.cloned.1.call-update) | async-done | bytes 192016
  1310.1 13.6 reduce-scatter.53.cloned.1.call-done
  1339.6 15.9 %reduce-scatter.45.cloned.1.call-done = bf16[384,288]{1,0:T(8,128)(2,1)} async-done(((bf16[768,288]{1,0:T(8,128)(2,1)}), bf16[384,288]{1,0:T(8,128)(2,1)}) %reduce-scatter.45.cloned.1.call-update) | async-done | bytes 221200
  (489 shorter events, 444.7 us)
Async XLA Ops:
  7.2 90.3 %all-gather.12.cloned.1.call-start = ((), (), s32[]{:S(2)}) async-start(), calls=%async_computation.14 | async-start | bytes 1671168 | tf_op jit(solution)/shard_map/all_gather | solution.py:130
  14.2 85.3 %all-gather.14.cloned.1.call-start = ((), (), s32[]{:S(2)}) async-start(), calls=%async_computation.15 | async-start | bytes 1671168 | tf_op jit(solution)/shard_map/all_gather | solution.py:131
  20.1 145.0 %all-gather.16.cloned.1.call-start = ((), (), s32[]{:S(2)}) async-start(), calls=%async_computation.16 | async-start | bytes 7520256 | tf_op jit(solution)/shard_map/all_gather | solution.py:132
  28.7 184.3 %all-gather.18.cloned.1.call-start = ((), (), s32[]{:S(2)}) async-start(), calls=%async_computation.17 | async-start | bytes 3760128 | tf_op jit(solution)/shard_map/all_gather | solution.py:133
  34.5 269.0 %all-gather.20.cloned.1.call-start = ((), (), s32[]{:S(2)}) async-start(), calls=%async_computation.18 | async-start | bytes 1253376 | tf_op jit(solution)/shard_map/all_gather | solution.py:134
  41.1 270.6 %all-gather.22.cloned.1.call-start = ((), (), s32[]{:S(2)}) async-start(), calls=%async_computation.19 | async-start | bytes 5013504 | tf_op jit(solution)/shard_map/all_gather | solution.py:135
  47.7 313.6 %all-gather.24.cloned.1.call-start = ((), (), s32[]{:S(2)}) async-start(), calls=%async_computation.20 | async-start | bytes 5013504 | tf_op jit(solution)/shard_map/all_gather | solution.py:136
  53.7 725.7 %reduce-scatter.37.cloned.1.call-start = ((), (), s32[]{:S(2)}) async-start(), calls=%async_computation.25 | async-start | bytes 1253376 | tf_op jit(solution)/shard_map/reduce_scatter | solution.py:323
  56.5 225.7 %copy-start.17 = (pred[256,256]{0,1:T(8,128)(4,1)}, pred[256,256]{0,1:T(8,128)(4,1)S(1)}, u32[]{:S(2)}) copy-start(pred[256,256]{0,1:T(8,128)(4,1)S(1)} %broadcast_compare_fusion) | copy-start | bytes 196612
  599.8 181.5 %reduce-scatter.31.cloned.1.call-start = ((), (), s32[]{:S(2)}) async-start(), calls=%async_computation.22 | async-start | bytes 1671168 | tf_op jit(solution)/shard_map/reduce_scatter | solution.py:314
  695.6 121.2 %reduce-scatter.29.cloned.1.call-start = ((), (), s32[]{:S(2)}) async-start(), calls=%async_computation.21 | async-start | bytes 1671168 | tf_op jit(solution)/shard_map/reduce_scatter | solution.py:311
  698.4 189.5 %reduce-scatter.35.cloned.1.call-start = ((), (), s32[]{:S(2)}) async-start(), calls=%async_computation.24 | async-start | bytes 3760128 | tf_op jit(solution)/shard_map/reduce_scatter | solution.py:320
  718.2 247.9 %reduce-scatter.39.cloned.1.call-start = ((), (), s32[]{:S(2)}) async-start(), calls=%async_computation.26 | async-start | bytes 5013504 | tf_op jit(solution)/shard_map/reduce_scatter | solution.py:326
  731.3 313.8 %reduce-scatter.41.cloned.1.call-start = ((), (), s32[]{:S(2)}) async-start(), calls=%async_computation.27 | async-start | bytes 5013504 | tf_op jit(solution)/shard_map/reduce_scatter | solution.py:329
  741.9 396.1 %reduce-scatter.33.cloned.1.call-start = ((), (), s32[]{:S(2)}) async-start(), calls=%async_computation.23 | async-start | bytes 7520256 | tf_op jit(solution)/shard_map/reduce_scatter | solution.py:317
  747.0 448.5 %reduce-scatter.47.cloned.1.call-start = ((), (), s32[]{:S(2)}) async-start(), calls=%async_computation.30 | async-start | bytes 208896
  777.8 267.6 %copy-start.65 = (f32[1024]{0:T(1024)S(1)}, f32[1024]{0:T(1024)}, u32[]{:S(2)}) copy-start(f32[1024]{0:T(1024)} %copy-done.64) | copy-start | bytes 12292
  777.8 477.2 %reduce-scatter.55.cloned.1.call-start = ((), (), s32[]{:S(2)}) async-start(), calls=%async_computation.34 | async-start | bytes 835584
  779.4 488.2 %reduce-scatter.51.cloned.1.call-start = ((), (), s32[]{:S(2)}) async-start(), calls=%async_computation.32 | async-start | bytes 294912
  781.2 511.1 %all-reduce.74.cloned.1.call-start = ((), (), s32[]{:S(2)}) async-start(), calls=%async_computation.35 | async-start | bytes 393216
  816.9 491.4 %reduce-scatter.49.cloned.1.call-start = ((), (), s32[]{:S(2)}) async-start(), calls=%async_computation.31 | async-start | bytes 589824
  889.7 433.9 %reduce-scatter.53.cloned.1.call-start = ((), (), s32[]{:S(2)}) async-start(), calls=%async_computation.33 | async-start | bytes 589824
  968.0 370.0 %reduce-scatter.43.cloned.1.call-start = ((), (), s32[]{:S(2)}) async-start(), calls=%async_computation.28 | async-start | bytes 442368 | tf_op jit(solution)/shard_map/reduce_scatter | solution.py:358
  1045.1 310.4 %reduce-scatter.45.cloned.1.call-start = ((), (), s32[]{:S(2)}) async-start(), calls=%async_computation.29 | async-start | bytes 884736
  (133 other events, 3380.3 us)
Sparse Core Ops, SparseCore 0:
  14.3 41.3 all-gather.11
  58.6 38.7 all-gather.13
  99.7 65.4 all-gather.15
  167.3 45.6 all-gather.17
  215.1 37.3 all-gather.19
  254.6 52.3 all-gather.21
  309.3 51.9 all-gather.23
  599.9 56.6 reduce-scatter.36
  695.7 58.0 reduce-scatter.30
  758.3 58.4 reduce-scatter.28
  820.7 67.0 reduce-scatter.34
  891.5 74.4 reduce-scatter.38
  970.4 74.6 reduce-scatter.40
  1048.9 89.0 reduce-scatter.32
  1142.4 53.0 reduce-scatter.46
  1199.3 55.5 reduce-scatter.54
  1257.6 9.9 reduce-scatter.50
  1269.8 22.4 all-reduce.73
  1295.1 13.1 reduce-scatter.48
  1310.5 13.1 reduce-scatter.52
  1325.9 12.0 reduce-scatter.42
  1340.2 15.2 reduce-scatter.44
where the time goes:
time: 1380 us; the launch traced here: 1360 us
  waiting for transfers between devices  637 us (46%)
  other arithmetic  229 us (17%)
  matrix products  210 us (15%)
  local copies, waits for them, and re-layouts  176 us (13%)
  blocking collectives  92.9 us (7%)
  between operations  18.2 us (1%)
    unnamed x29, waiting for transfers between devices  178 us
    dot_general x5, matrix products, against(): lax.dot_general(left, right, (((1,), (1,)), ((), ())), preferred_element_...  93.4 us
    reduce_scatter x1, waiting for transfers between devices, body(): lax.psum_scatter(mod_term.astype(jnp.bfloat16), 'dp', scatter_dimension=1...  87.5 us
    reduce_scatter x1, waiting for transfers between devices, body(): lax.psum_scatter(expand_term.astype(jnp.bfloat16), 'dp', scatter_dimensio...  76.3 us
    reduce_scatter x1, waiting for transfers between devices, body(): lax.psum_scatter(shrink_term.astype(jnp.bfloat16), 'dp', scatter_dimensio...  75.8 us
    reduce_scatter x1, waiting for transfers between devices, body(): lax.psum_scatter(qkv_term.astype(jnp.bfloat16), 'dp', scatter_dimension=1...  70.9 us
    all_gather x1, waiting for transfers between devices, fetch_forward(): lax.all_gather(gathered[2], 'dp', axis=1, tiled=True)  63.7 us
    convert_element_type x5, local copies, waits for them, and re-layouts, body(): d_qkv = from_groups(stacked).astype(jnp.bfloat16)  61.8 us
  transfers between devices with their start and end apart: 22, of which 16 were waited for; matrix products, arithmetic and copies ran while one was open for 27% of the time, Pallas kernels for 0%

commit v1 on v0

--- a/solution.py
+++ b/solution.py
@@ -10,6 +10,19 @@
 CLASSES = 1000
 SIDE = 32
 GROUP = 256
+
+
+def collect(x, axis, dim):
+    ways = lax.axis_size(axis)
+    up = [(d, (d + 1) % ways) for d in range(ways)]
+    down = [(d, (d - 1) % ways) for d in range(ways)]
+    earlier, later = ([x], [x])
+    for _ in range(ways // 2):
+        earlier.append(lax.ppermute(earlier[-1], axis, up))
+    for _ in range((ways - 1) // 2):
+        later.append(lax.ppermute(later[-1], axis, down))
+    line = jnp.concatenate([*earlier[::-1], *later[1:]], axis=dim)
+    return jnp.roll(line, (lax.axis_index(axis) - ways // 2) * x.shape[dim], axis=dim)
 
 
 def token_items(size_tag):
@@ -129,7 +142,7 @@
     return (
         lax.all_gather(gathered[0], "dp", axis=1, tiled=True),
         lax.all_gather(gathered[1], "dp", axis=1, tiled=True),
-        lax.all_gather(gathered[2], "dp", axis=1, tiled=True),
+        collect(gathered[2], "dp", 1),
         lax.all_gather(gathered[3], "dp", axis=1, tiled=True),
         lax.all_gather(gathered[4], "dp", axis=1, tiled=True),
         lax.all_gather(gathered[5], "dp", axis=1, tiled=True),

time: 1380 us -> 1360 us (0.986)
  waiting for transfers between devices: 637 us -> 543 us
  starting transfers between devices: 1.29 us -> 53.3 us
  local copies, waits for them, and re-layouts: 176 us -> 198 us
    reduce_scatter x1, waiting for transfers between devices: 70.9 us -> 0.02 us  [body(): lax.psum_scatter(qkv_term.astype(jnp.bfloat16), 'dp', scatter_dimension=1...]
    all_gather x1, waiting for transfers between devices: 63.7 us -> 0.02 us  [fetch_again(): lax.all_gather(gathered[0], 'dp', axis=1, tiled=True)]
    ppermute x0 -> x15, starting transfers between devices: none -> 51.9 us  [the longest x8 29.1 us: collect(): earlier.append(lax.ppermute(earlier[-1], axis, up))]
    all_gather x1, waiting for transfers between devices: 29.4 us -> 0.02 us  [fetch_forward(): lax.all_gather(gathered[3], 'dp', axis=1, tiled=True)]
    ppermute x0 -> x15, waiting for transfers between devices: none -> 28.4 us  [the longest x8 23.8 us: collect(): earlier.append(lax.ppermute(earlier[-1], axis, up))]
    reduce_scatter x1, waiting for transfers between devices: 35.6 us -> 63.3 us  [body(): lax.psum_scatter(step_term.astype(jnp.bfloat16), 'dp', scatter_dimension=...]
    unnamed x288 -> x321, local copies, waits for them, and re-layouts: 40.3 us -> 62.2 us
    reduce_scatter x1, waiting for transfers between devices: 0.02 us -> 19.9 us  [body(): lax.psum_scatter(class_term.astype(jnp.bfloat16), 'dp', scatter_dimension...]
  transfers between devices with their start and end apart: 22 -> 37, of which waited for: 16 -> 22; matrix products, arithmetic and copies ran while one was open for 27% -> 46% of each run, Pallas kernels for 0% -> 0%
where the time goes in v1:
time: 1360 us; the launch traced here: 1350 us
  waiting for transfers between devices  543 us (40%)
  other arithmetic  227 us (17%)
  matrix products  214 us (16%)
  local copies, waits for them, and re-layouts  198 us (15%)
  blocking collectives  97.1 us (7%)
  starting transfers between devices  53.3 us (4%)
  between operations  18.4 us (1%)
    unnamed x29, waiting for transfers between devices  178 us
    dot_general x5, matrix products, against(): lax.dot_general(left, right, (((1,), (1,)), ((), ())), preferred_element_...  96 us
    reduce_scatter x1, waiting for transfers between devices, body(): lax.psum_scatter(mod_term.astype(jnp.bfloat16), 'dp', scatter_dimension=1...  87.5 us
    reduce_scatter x1, waiting for transfers between devices, body(): lax.psum_scatter(expand_term.astype(jnp.bfloat16), 'dp', scatter_dimensio...  78.2 us
    reduce_scatter x1, waiting for transfers between devices, body(): lax.psum_scatter(shrink_term.astype(jnp.bfloat16), 'dp', scatter_dimensio...  75.7 us
    reduce_scatter x1, waiting for transfers between devices, body(): lax.psum_scatter(step_term.astype(jnp.bfloat16), 'dp', scatter_dimension=...  63.3 us
    unnamed x321, local copies, waits for them, and re-layouts  62.2 us
    convert_element_type x5, local copies, waits for them, and re-layouts, body(): d_qkv = from_groups(stacked).astype(jnp.bfloat16)  61.5 us
  transfers between devices with their start and end apart: 37, of which 22 were waited for; matrix products, arithmetic and copies ran while one was open for 46% of the time, Pallas kernels for 0%

profile of v1, /device:TPU:0, one launch (start us, length us, event | category | flops | bytes accessed | tf_op | source)
XLA Modules:
  0.0 1351.5 jit_solution(1656992339171687182)
XLA Ops:
  56.5 22.1 %all-gather.2 = bf16[16,48,9]{1,2,0:T(8,128)(2,1)S(1)} all-gather(bf16[1,48,9]{1,2,0:T(8,128)(2,1)S(1)} %bitcast.227), channel_id=1, replica_groups=mesh['dp'=16,'fsdp'=2] {'dp'}, dimensions={0}, use_global_device_ids=true | all-gather | bytes 14688 | tf_op jit(solution)/shard_map/all_gather | solution.py:150
  78.8 20.5 %all-gather.3 = bf16[16,192,9]{1,2,0:T(8,128)(2,1)S(1)} all-gather(bf16[1,192,9]{1,2,0:T(8,128)(2,1)S(1)} %bitcast.226), channel_id=1, replica_groups=mesh['dp'=16,'fsdp'=2] {'dp'}, dimensions={0}, use_global_device_ids=true | all-gather | bytes 58752 | tf_op jit(solution)/shard_map/all_gather | solution.py:151
  243.5 15.0 %reshape_reshape.8 = bf16[4,256,3,12,64]{4,3,2,1,0:T(8,128)(2,1)} reshape(bf16[2,2,16,16,2304]{4,3,2,1,0:T(8,128)(2,1)} %bitcast.183) | data formatting | bytes 9437184 | tf_op jit(solution)/shard_map/reshape;reshape | solution.py:241
  333.2 22.2 %multiply_add_fusion = f32[32,32,3072]{2,1,0:T(8,128)} fusion(f32[32,32,3072]{2,1,0:T(8,128)S(1)} %bitcast.177, f32[3072]{0:T(1024)S(1)} %bitcast.197, f32[32,32]{1,0:T(8,128)S(1)} %get-tuple-element.159, f32[3072]{0:T(1024)S(1)} %bitcast.199, f32[32,32]{1,0:T(8,128)S(1)} %get-tuple-element.154, f32[3072]{0:T(1024)S(1)} %bitcast.201, ...), kind=kLoop, calls=%fused_computation.57 | loop fusion | flops 81788928 | bytes 25313280 | tf_op jit(solution)/shard_map/jvp()/add | solution.py:56
  355.4 63.3 %multiply_reduce_fusion.8 = (f32[3072]{0:T(1024)}, f32[3072]{0:T(1024)}, f32[3072]{0:T(1024)}, f32[3072]{0:T(1024)}, f32[3072]{0:T(1024)}, /*index=5*/f32[3072]{...) fusion(f32[32,32,3072]{2,1,0:T(8,128)} %bitcast.178, f32[32,32]{1,0:T(8,128)S(1)} %get-tuple-element.159, ...), kind=kOutput, calls=%fused_computation.44 | convolution fusion | flops 4971798528 | bytes 44186624 | tf_op jit(solution)/shard_map/dot_general | solution.py:110
  418.7 42.0 %multiply_multiply_fusion.10 = (f32[32,32,3072]{2,1,0:T(8,128)}, f32[32,32,3072]{2,1,0:T(8,128)}, f32[32,32,3072]{2,1,0:T(8,128)}, f32[32,32,3072]{2,1,0:T(8,128...) fusion(f32[32,32,3072]{2,1,0:T(8,128)} %bitcast.176, ...), kind=kLoop, calls=%fused_computation.56 | loop fusion | flops 56623104 | bytes 125976576 | tf_op jit(solution)/shard_map/transpose(jvp())/mul | solution.py:56
  460.8 23.6 %pad_add_fusion = f32[34,34,3072]{2,1,0:T(8,128)} fusion(f32[32,32,3072]{2,1,0:T(8,128)} %get-tuple-element.116, f32[32,32,3072]{2,1,0:T(8,128)} %get-tuple-element.117, f32[32,32,3072]{2,1,0:T(8,128)} %get-tuple-element.118, f32[32,32,3072]{2,1,0:T(8,128)} %get-tuple-element.110), kind=kLoop, calls=%fused_computation.10 | loop fusion | flops 10653696 | bytes 64536576 | tf_op jit(solution)/shard_map/transpose(jvp())/add_any | solution.py:54
  484.3 31.7 %fusion.14 = bf16[32,32,3072]{2,1,0:T(8,128)(2,1)} fusion(f32[32,32,3072]{2,1,0:T(8,128)} %get-tuple-element.111, f32[32,32,3072]{2,1,0:T(8,128)} %get-tuple-element.112, f32[32,32,3072]{2,1,0:T(8,128)} %get-tuple-element.113, f32[32,32,3072]{2,1,0:T(8,128)} %get-tuple-element.114, f32[32,32,3072]{2,1,0:T(8,128)} %get-tuple-element.115, ...), kind=kLoop, calls=%fused_computation.26 | loop fusion | flops 18874368 | bytes 81788928 | tf_op jit(solution)/shard_map/convert
  533.2 13.6 %fusion.88 = (f32[1024]{0:T(1024)S(1)}, f32[1024,768]{1,0:T(8,128)S(1)}, f32[1024,768]{1,0:T(8,128)}, bf16[1024,768]{1,0:T(8,128)(2,1)}, f32[1024,768]{1,0:T(8,128)}) fusion(f32[1024]{0:T(1024)S(1)} %multiply_multiply_fusion.22, f32[1024,768]{1,0:T(8,128)S(1)} %copy-done.19, f32[1024]{0:T(1024)S(1)} %broadcast_multiply_fusion.9, f32[1024]{0:T(1024)S(1)} %fusion.74, ...), kind=kOutput, calls=%fused_computation.340 | convolution fusion | flops 4846779392 | bytes 28355584 | tf_op jit(solution)/shard_map/dot_general | solution.py:261
  609.6 15.0 %copy.106 = bf16[4,256,3,12,64]{4,3,2,1,0:T(8,128)(2,1)} copy(bf16[4,256,3,12,64]{1,4,3,0,2:T(8,128)(2,1)} %maximum_convert_fusion) | data formatting | bytes 9437184 | tf_op jit(solution)/shard_map/convert_element_type | solution.py:296
  624.7 15.6 %convert_element_type.240 = bf16[2,2,16,16,2304]{4,3,2,1,0:T(8,128)(2,1)} reshape(bf16[4,256,3,12,64]{4,3,2,1,0:T(8,128)(2,1)} %copy.106) | data formatting | bytes 9437184 | tf_op jit(solution)/shard_map/convert_element_type | solution.py:296
  681.2 13.7 %multiply_multiply_fusion.19 = (f32[32,32,768]{2,1,0:T(8,128)}, f32[32,32,768]{2,1,0:T(8,128)S(1)}, f32[32,32,768]{2,1,0:T(8,128)S(1)}, f32[32,32,768]{2,1,0:T(8...) fusion(f32[768]{0:T(1024)S(1)} %copy-done.73, ...), kind=kOutput, calls=%fused_computation.162 | convolution fusion | flops 3638034432 | bytes 39779328 | tf_op jit(solution)/shard_map/dot_general | solution.py:110
  756.0 19.1 %multiply_reduce_fusion.18 = (f32[768]{0:T(1024)S(1)}, f32[768]{0:T(1024)S(1)}, f32[768]{0:T(1024)S(1)}, f32[768]{0:T(1024)S(1)}, f32[768]{0:T(1024)S(1)}, /*ind...) fusion(f32[32,32,768]{2,1,0:T(8,128)} %get-tuple-element.167, f32[32,32,768]{2,1,0:T(8,128)} %bitcast.182, ...), kind=kLoop, calls=%fused_computation.128 | loop fusion | flops 30663936 | bytes 7964672 | tf_op jit(solution)/shard_map/transpose(jvp())/reduce_sum | solution.py:56
  791.3 19.9 %reduce-scatter.31.cloned.1.call-done = bf16[1000,48]{0,1:T(8,128)(2,1)} async-done(((bf16[1000,768]{0,1:T(8,128)(2,1)}), bf16[1000,48]{0,1:T(8,128)(2,1)}) %reduce-scatter.31.cloned.1.call-update) | async-done | bytes 96016 | tf_op jit(solution)/shard_map/reduce_scatter | solution.py:327
  811.2 63.3 %reduce-scatter.29.cloned.1.call-done = bf16[1000,48]{0,1:T(8,128)(2,1)} async-done(((bf16[1000,768]{0,1:T(8,128)(2,1)}), bf16[1000,48]{0,1:T(8,128)(2,1)}) %reduce-scatter.29.cloned.1.call-update) | async-done | bytes 96016 | tf_op jit(solution)/shard_map/reduce_scatter | solution.py:324
  874.6 78.2 %reduce-scatter.39.cloned.1.call-done = bf16[768,192]{0,1:T(8,128)(2,1)} async-done(((bf16[768,3072]{0,1:T(8,128)(2,1)}), bf16[768,192]{0,1:T(8,128)(2,1)}) %reduce-scatter.39.cloned.1.call-update) | async-done | bytes 294928 | tf_op jit(solution)/shard_map/reduce_scatter | solution.py:339
  956.0 75.7 %reduce-scatter.41.cloned.1.call-done = bf16[3072,48]{0,1:T(8,128)(2,1)} async-done(((bf16[3072,768]{0,1:T(8,128)(2,1)}), bf16[3072,48]{0,1:T(8,128)(2,1)}) %reduce-scatter.41.cloned.1.call-update) | async-done | bytes 294928 | tf_op jit(solution)/shard_map/reduce_scatter | solution.py:342
  1037.3 87.5 %reduce-scatter.33.cloned.1.call-done = bf16[768,288]{0,1:T(8,128)(2,1)} async-done(((bf16[768,4608]{0,1:T(8,128)(2,1)}), bf16[768,288]{0,1:T(8,128)(2,1)}) %reduce-scatter.33.cloned.1.call-update) | async-done | bytes 442384 | tf_op jit(solution)/shard_map/reduce_scatter | solution.py:330
  1132.0 50.3 %reduce-scatter.47.cloned.1.call-done = bf16[48,9]{1,0:T(8,128)(2,1)} async-done(((bf16[768,9]{1,0:T(8,128)(2,1)}), bf16[48,9]{1,0:T(8,128)(2,1)}) %reduce-scatter.47.cloned.1.call-update) | async-done | bytes 880
  1183.1 58.7 %reduce-scatter.55.cloned.1.call-done = bf16[192,9]{1,0:T(8,128)(2,1)} async-done(((bf16[3072,9]{1,0:T(8,128)(2,1)}), bf16[192,9]{1,0:T(8,128)(2,1)}) %reduce-scatter.55.cloned.1.call-update) | async-done | bytes 3472
  1256.0 14.2 %reduce-scatter.49.cloned.1.call-done = bf16[384,144]{1,0:T(8,128)(2,1)} async-done(((bf16[768,144]{1,0:T(8,128)(2,1)}), bf16[384,144]{1,0:T(8,128)(2,1)}) %reduce-scatter.49.cloned.1.call-update) | async-done | bytes 110608
  1271.9 23.2 %all-reduce.74.cloned.1.call-done = (bf16[1000,48]{0,1:T(8,128)(2,1)}, bf16[1000,48]{0,1:T(8,128)(2,1)}) async-done(((bf16[1000,48]{0,1:T(8,128)(2,1)}, bf16[1000,48]{0,1:T(8,128)(2,1)}), (bf16[1000,48]{0,1:T(8,128)(2,1)}, bf16[1000,48]{0,1:T(8,128)(2,1)})) %all-reduce.74.cloned.1.call-update) | async-done | bytes 192016
  1312.2 12.5 reduce-scatter.43.cloned.1.call-done
  1326.4 15.9 %reduce-scatter.45.cloned.1.call-done = bf16[384,288]{1,0:T(8,128)(2,1)} async-done(((bf16[768,288]{1,0:T(8,128)(2,1)}), bf16[384,288]{1,0:T(8,128)(2,1)}) %reduce-scatter.45.cloned.1.call-update) | async-done | bytes 221200
  (552 shorter events, 516.3 us)
Async XLA Ops:
  7.2 173.4 %all-gather.12.cloned.1.call-start = ((), (), s32[]{:S(2)}) async-start(), calls=%async_computation.14 | async-start | bytes 1671168 | tf_op jit(solution)/shard_map/all_gather | solution.py:143
  14.2 168.3 %all-gather.14.cloned.1.call-start = ((), (), s32[]{:S(2)}) async-start(), calls=%async_computation.15 | async-start | bytes 1671168 | tf_op jit(solution)/shard_map/all_gather | solution.py:144
  20.1 199.9 %all-gather.16.cloned.1.call-start = ((), (), s32[]{:S(2)}) async-start(), calls=%async_computation.16 | async-start | bytes 3760128 | tf_op jit(solution)/shard_map/all_gather | solution.py:146
  27.4 283.5 %all-gather.18.cloned.1.call-start = ((), (), s32[]{:S(2)}) async-start(), calls=%async_computation.17 | async-start | bytes 1253376 | tf_op jit(solution)/shard_map/all_gather | solution.py:147
  32.5 286.1 %all-gather.20.cloned.1.call-start = ((), (), s32[]{:S(2)}) async-start(), calls=%async_computation.18 | async-start | bytes 5013504 | tf_op jit(solution)/shard_map/all_gather | solution.py:148
  40.6 314.8 %all-gather.22.cloned.1.call-start = ((), (), s32[]{:S(2)}) async-start(), calls=%async_computation.19 | async-start | bytes 5013504 | tf_op jit(solution)/shard_map/all_gather | solution.py:149
  48.4 668.5 %all-gather.24.cloned.1.call-start = ((), (), s32[]{:S(2)}) async-start(), calls=%async_computation.20 | async-start | bytes 7520256 | tf_op jit(solution)/shard_map/all_gather | solution.py:164
  55.1 45.6 %collective-permute-start.8 = (bf16[768,288]{0,1:T(8,128)(2,1)S(1)}, bf16[768,288]{0,1:T(8,128)(2,1)S(1)}, u32[]{:S(2)}, u32[]{:S(2)}) collective-permute-start(bf16[768,288]{0,1:T(8,128)(2,1)S(1)} %all_gather.61), channel_id=1, source_target_pairs={{0,30},{2,0},{4,2},{6,4},{8,6},{10,8},{12,10},{14,12},{16,14},{18,... | collective-permute-start | bytes 1327112 | tf_op jit(solution)/shard_map/ppermute | solution.py:23
  55.1 44.4 %collective-permute-start = (bf16[768,288]{0,1:T(8,128)(2,1)S(1)}, bf16[768,288]{0,1:T(8,128)(2,1)S(1)}, u32[]{:S(2)}, u32[]{:S(2)}) collective-permute-start(bf16[768,288]{0,1:T(8,128)(2,1)S(1)} %all_gather.61), channel_id=1, source_target_pairs={{0,2},{2,4},{4,6},{6,8},{8,10},{10,12},{12,14},{14,16},{16,18},{18... | collective-permute-start | bytes 1327112 | tf_op jit(solution)/shard_map/ppermute | solution.py:21
  55.8 731.8 %reduce-scatter.37.cloned.1.call-start = ((), (), s32[]{:S(2)}) async-start(), calls=%async_computation.25 | async-start | bytes 1253376 | tf_op jit(solution)/shard_map/reduce_scatter | solution.py:336
  593.6 195.8 %reduce-scatter.35.cloned.1.call-start = ((), (), s32[]{:S(2)}) async-start(), calls=%async_computation.24 | async-start | bytes 3760128 | tf_op jit(solution)/shard_map/reduce_scatter | solution.py:333
  680.6 130.7 %reduce-scatter.31.cloned.1.call-start = ((), (), s32[]{:S(2)}) async-start(), calls=%async_computation.22 | async-start | bytes 1671168 | tf_op jit(solution)/shard_map/reduce_scatter | solution.py:327
  723.8 150.7 %reduce-scatter.29.cloned.1.call-start = ((), (), s32[]{:S(2)}) async-start(), calls=%async_computation.21 | async-start | bytes 1671168 | tf_op jit(solution)/shard_map/reduce_scatter | solution.py:324
  726.5 226.3 %reduce-scatter.39.cloned.1.call-start = ((), (), s32[]{:S(2)}) async-start(), calls=%async_computation.26 | async-start | bytes 5013504 | tf_op jit(solution)/shard_map/reduce_scatter | solution.py:339
  739.0 292.8 %reduce-scatter.41.cloned.1.call-start = ((), (), s32[]{:S(2)}) async-start(), calls=%async_computation.27 | async-start | bytes 5013504 | tf_op jit(solution)/shard_map/reduce_scatter | solution.py:342
  750.1 374.7 %reduce-scatter.33.cloned.1.call-start = ((), (), s32[]{:S(2)}) async-start(), calls=%async_computation.23 | async-start | bytes 7520256 | tf_op jit(solution)/shard_map/reduce_scatter | solution.py:330
  755.2 427.1 %reduce-scatter.47.cloned.1.call-start = ((), (), s32[]{:S(2)}) async-start(), calls=%async_computation.30 | async-start | bytes 208896
  786.0 455.8 %reduce-scatter.55.cloned.1.call-start = ((), (), s32[]{:S(2)}) async-start(), calls=%async_computation.34 | async-start | bytes 835584
  787.5 466.8 %reduce-scatter.51.cloned.1.call-start = ((), (), s32[]{:S(2)}) async-start(), calls=%async_computation.32 | async-start | bytes 294912
  789.3 480.8 %reduce-scatter.49.cloned.1.call-start = ((), (), s32[]{:S(2)}) async-start(), calls=%async_computation.31 | async-start | bytes 589824
  791.3 503.8 %all-reduce.74.cloned.1.call-start = ((), (), s32[]{:S(2)}) async-start(), calls=%async_computation.35 | async-start | bytes 393216
  874.5 435.9 %reduce-scatter.53.cloned.1.call-start = ((), (), s32[]{:S(2)}) async-start(), calls=%async_computation.33 | async-start | bytes 589824
  954.7 370.0 %reduce-scatter.43.cloned.1.call-start = ((), (), s32[]{:S(2)}) async-start(), calls=%async_computation.28 | async-start | bytes 442368 | tf_op jit(solution)/shard_map/reduce_scatter | solution.py:371
  1031.8 310.5 %reduce-scatter.45.cloned.1.call-start = ((), (), s32[]{:S(2)}) async-start(), calls=%async_computation.29 | async-start | bytes 884736
  (149 other events, 3443.7 us)
Sparse Core Ops, SparseCore 0:
  14.3 41.4 all-gather.11
  58.6 38.9 all-gather.13
  99.9 61.1 all-gather.15
  163.2 40.0 all-gather.17
  205.5 52.2 all-gather.19
  259.9 51.9 all-gather.21
  314.1 65.1 all-gather.23
  593.7 58.6 reduce-scatter.36
  680.7 68.6 reduce-scatter.34
  752.9 58.2 reduce-scatter.30
  815.9 58.5 reduce-scatter.28
  878.2 74.5 reduce-scatter.38
  957.1 74.5 reduce-scatter.40
  1035.6 89.1 reduce-scatter.32
  1129.1 53.1 reduce-scatter.46
  1186.1 55.5 reduce-scatter.54
  1244.4 9.8 reduce-scatter.50
  1257.0 13.1 reduce-scatter.48
  1272.6 22.4 all-reduce.73
  1297.3 13.1 reduce-scatter.52
  1312.7 12.0 reduce-scatter.42
  1327.0 15.2 reduce-scatter.44
